TPU v7x, 32 devices: a whole 2x2x4 slice. The times are simulated.
32 devices in a mesh: pix: 16 (over z, y, x), lat: 2 (over core).
Axes of the slice: x: 2, y: 2, z: 4, core: 2. Of those that a mesh axis runs over, the one named last changes fastest.
Arguments:
- latents: bfloat16 [8192, 512], P('pix'), may hold values from -6 to 6
- w_send: bfloat16 [512, 512], P(None, 'lat'), may hold values from -0.25 to 0.25
- w_recv: bfloat16 [512, 512], P(None, 'lat'), may hold values from -0.25 to 0.25
- edge_bias: float32 [512], P('lat'), may hold values from -3 to 3
- w_msg: bfloat16 [512, 512], P('lat'), may hold values from -0.25 to 0.25
- w_self: bfloat16 [512, 512], P(None, 'lat'), may hold values from -0.25 to 0.25
- w_agg: bfloat16 [512, 512], P(None, 'lat'), may hold values from -0.25 to 0.25
- node_bias: float32 [512], P('lat'), may hold values from -3 to 3
- w_node: bfloat16 [512, 512], P('lat'), may hold values from -0.25 to 0.25
- norm_gain: float32 [512], replicated, may hold values from 0.25 to 1.75
- coarse_ids: int32 [128], P('pix'), may hold values from 0 to 511
- send_list: int32 [16], P('pix'), may hold values from 0 to 3
- recv_tile: int32 [512], P('pix'), may hold values from 0 to 3
- send_tile: int32 [512], P('pix'), may hold values from 0 to 6, as said below
- edge_ends: int32 [512, 2, 128], P('pix'), may hold values from 0 to 127
- edge_mask: int32 [512, 128], P('pix'), may hold values 0 or 1
- cotangent: bfloat16 [8192, 512], P('pix'), may hold values from -6 to 6
Outputs:
- new_latents: bfloat16 [8192, 512], P('pix')
- grad_latents: float32 [8192, 512], P('pix', 'lat')
- grad_w_send: float32 [512, 512], P(None, 'lat')
- grad_w_recv: float32 [512, 512], P(None, 'lat')
- grad_edge_bias: float32 [512], P('lat')
- grad_w_msg: float32 [512, 512], P('lat')
- grad_w_self: float32 [512, 512], P(None, 'lat')
- grad_w_agg: float32 [512, 512], P(None, 'lat')
- grad_node_bias: float32 [512], P('lat')
- grad_w_node: float32 [512, 512], P('lat')
- grad_gain: float32 [512], replicated
Inputs may be any that keep to these rules, and one draw needn't show every extreme that they name: `send_tile`: a block's sender tile, numbered as in the first step: first the device's own tiles, then the 1 lent tiles of the preceding and of the following pixel range, then the 1 tiles of the coarse panel; in each device's own run of 32 blocks, the first names a tile lent by the preceding range and the second one lent by the following range. `coarse_ids`: rows may repeat.
All inputs are finite; a program needn't handle non-finite values. No bound on the sum of `edge_mask` on one device may be relied on, other than what follows from the above.
Results may differ from a plain program's by a relative error of at most 0.0085.
Values may be sent and summed in bfloat16 or wider, within the bound.
A program may use at most 128 MiB of HBM per device.

v0:
```python
import math
import jax
import jax.numpy as jnp
from jax import lax
from jax.sharding import PartitionSpec as P

norm_eps = 1e-05


def from_behind(block, axis, distance):
    devices = range(lax.axis_size(axis))
    route = [((i - distance) % len(devices), i) for i in devices]
    return lax.ppermute(block, axis, route)


def silu_slope(values):
    sigma = jax.nn.sigmoid(values)
    return sigma * (1.0 + values * (1.0 - sigma))


def tile_sums(values, offsets, weights, block_tiles, tile_count):
    block_count, tile_len = offsets.shape
    width = values.shape[-1]
    positions = jnp.arange(tile_len, dtype=jnp.int32)
    incidence = (offsets[:, :, None] == positions[None, None, :]).astype(jnp.float32) * weights[
        :, :, None
    ]
    per_block = jnp.einsum(
        "ben,beh->bnh",
        incidence,
        values.reshape(block_count, tile_len, width),
        precision=lax.Precision.HIGHEST,
    )
    tile_ids = jnp.arange(tile_count, dtype=jnp.int32)
    selector = (block_tiles[None, :] == tile_ids[:, None]).astype(jnp.float32)
    summed = jnp.einsum("tb,bnh->tnh", selector, per_block, precision=lax.Precision.HIGHEST)
    return summed.reshape(tile_count * tile_len, width)


def shards(
    latents,
    w_send,
    w_recv,
    edge_bias,
    w_msg,
    w_self,
    w_agg,
    node_bias,
    w_node,
    norm_gain,
    coarse_ids,
    send_list,
    recv_tile,
    send_tile,
    edge_ends,
    edge_mask,
    cotangent,
):
    node_dev, latent_width = latents.shape
    tile_len = edge_ends.shape[2]
    tiles_dev = node_dev // tile_len
    halo_rows = send_list.shape[0] * tile_len
    pix_count = lax.axis_size("pix")
    lat_count = lax.axis_size("lat")
    grad_scale = 1.0 / math.sqrt(node_dev * pix_count)
    hidden_part = w_send.shape[1]
    send_proj = jnp.dot(latents, w_send, preferred_element_type=jnp.float32)
    recv_proj = jnp.dot(latents, w_recv, preferred_element_type=jnp.float32)
    lent_rows = latents.reshape(tiles_dev, tile_len, latent_width)[send_list].reshape(
        halo_rows, latent_width
    )
    from_left = from_behind(lent_rows, "pix", 1)
    from_right = from_behind(lent_rows, "pix", -1)
    side_proj = jnp.dot(
        jnp.concatenate([from_left, from_right], axis=0), w_send, preferred_element_type=jnp.float32
    )
    panel_proj = jnp.dot(
        lax.all_gather(latents[coarse_ids], "pix", axis=0, tiled=True),
        w_send,
        preferred_element_type=jnp.float32,
    )
    source_proj = jnp.concatenate([send_proj, side_proj, panel_proj], axis=0)
    source_tiles = source_proj.shape[0] // tile_len
    sender_offs = edge_ends[:, 0, :]
    receiver_offs = edge_ends[:, 1, :]
    senders = (send_tile[:, None] * tile_len + sender_offs).reshape(-1)
    receivers = (recv_tile[:, None] * tile_len + receiver_offs).reshape(-1)
    mask_rows = edge_mask.astype(jnp.float32)
    edge_weight = mask_rows.reshape(-1)
    unit_rows = jnp.ones_like(mask_rows)
    edge_pre = source_proj[senders] + recv_proj[receivers] + edge_bias
    edge_act = jax.nn.silu(edge_pre).astype(jnp.bfloat16)
    message = jnp.dot(edge_act, w_msg, preferred_element_type=jnp.float32)
    agg_part = tile_sums(message, receiver_offs, mask_rows, recv_tile, tiles_dev)
    aggregate = lax.psum(agg_part, "lat")
    aggregate_bf = aggregate.astype(jnp.bfloat16)
    node_pre = (
        jnp.dot(latents, w_self, preferred_element_type=jnp.float32)
        + jnp.dot(aggregate_bf, w_agg, preferred_element_type=jnp.float32)
        + node_bias
    )
    node_act = jax.nn.silu(node_pre).astype(jnp.bfloat16)
    out_part = jnp.dot(node_act, w_node, preferred_element_type=jnp.float32)
    node_out = lax.psum(out_part, "lat")
    row_mean = jnp.mean(node_out, axis=-1, keepdims=True)
    centered = node_out - row_mean
    row_var = jnp.mean(centered * centered, axis=-1, keepdims=True)
    inv_std = lax.rsqrt(row_var + norm_eps)
    normed = centered * inv_std
    new_latents = (latents.astype(jnp.float32) + normed * norm_gain).astype(jnp.bfloat16)
    grad_out = cotangent.astype(jnp.float32)
    gain_sum = jnp.sum(grad_out * normed, axis=0)
    d_normed = grad_out * norm_gain
    out_cot = inv_std * (
        d_normed
        - jnp.mean(d_normed, axis=-1, keepdims=True)
        - normed * jnp.mean(d_normed * normed, axis=-1, keepdims=True)
    )
    out_cot_bf = out_cot.astype(jnp.bfloat16)
    node_w_grad = jnp.dot(node_act.T, out_cot_bf, preferred_element_type=jnp.float32)
    node_pre_cot = jnp.dot(out_cot_bf, w_node.T, preferred_element_type=jnp.float32) * silu_slope(
        node_pre
    )
    node_bias_sum = jnp.sum(node_pre_cot, axis=0)
    node_pre_bf = node_pre_cot.astype(jnp.bfloat16)
    self_w_grad = jnp.dot(latents.T, node_pre_bf, preferred_element_type=jnp.float32)
    agg_w_grad = jnp.dot(aggregate_bf.T, node_pre_bf, preferred_element_type=jnp.float32)
    latent_part = jnp.dot(node_pre_bf, w_self.T, preferred_element_type=jnp.float32)
    agg_cot_part = jnp.dot(node_pre_bf, w_agg.T, preferred_element_type=jnp.float32)
    agg_cot = lax.psum(agg_cot_part, "lat")
    agg_cot_bf = agg_cot.astype(jnp.bfloat16)
    msg_cot = agg_cot_bf[receivers] * edge_weight.astype(jnp.bfloat16)[:, None]
    msg_w_grad = jnp.dot(edge_act.T, msg_cot, preferred_element_type=jnp.float32)
    pre_cot = jnp.dot(msg_cot, w_msg.T, preferred_element_type=jnp.float32) * silu_slope(edge_pre)
    edge_bias_sum = jnp.sum(pre_cot, axis=0)
    src_cot = tile_sums(pre_cot, sender_offs, unit_rows, send_tile, source_tiles)
    dst_cot = tile_sums(pre_cot, receiver_offs, unit_rows, recv_tile, tiles_dev)
    own_grad = src_cot[:node_dev]
    left_back = src_cot[node_dev : node_dev + halo_rows]
    right_back = src_cot[node_dev + halo_rows : node_dev + 2 * halo_rows]
    panel_part = src_cot[node_dev + 2 * halo_rows :]
    to_left_owner = from_behind(left_back.astype(jnp.bfloat16), "pix", -1).astype(left_back.dtype)
    to_right_owner = from_behind(right_back.astype(jnp.bfloat16), "pix", 1).astype(right_back.dtype)
    returned = (to_left_owner + to_right_owner).reshape(send_list.shape[0], tile_len, hidden_part)
    own_grad = own_grad.reshape(tiles_dev, tile_len, hidden_part).at[send_list].add(returned)
    own_grad = own_grad.reshape(node_dev, hidden_part)
    coarse_grad = lax.psum_scatter(panel_part, "pix", scatter_dimension=0, tiled=True)
    own_grad = own_grad.at[coarse_ids].add(coarse_grad)
    src_cot_bf = own_grad.astype(jnp.bfloat16)
    dst_cot_bf = dst_cot.astype(jnp.bfloat16)
    send_w_grad = jnp.dot(latents.T, src_cot_bf, preferred_element_type=jnp.float32)
    recv_w_grad = jnp.dot(latents.T, dst_cot_bf, preferred_element_type=jnp.float32)
    latent_part = (
        latent_part
        + jnp.dot(src_cot_bf, w_send.T, preferred_element_type=jnp.float32)
        + jnp.dot(dst_cot_bf, w_recv.T, preferred_element_type=jnp.float32)
    )
    share_width = latent_width // lat_count
    lat_index = lax.axis_index("lat")
    lat_share = lax.psum_scatter(
        latent_part.astype(jnp.bfloat16), "lat", scatter_dimension=1, tiled=True
    ).astype(jnp.float32)
    grad_latents = lat_share + lax.dynamic_slice_in_dim(
        grad_out, lat_index * share_width, share_width, 1
    )
    summed = lax.psum(
        (
            send_w_grad,
            recv_w_grad,
            edge_bias_sum,
            msg_w_grad,
            self_w_grad,
            agg_w_grad,
            node_bias_sum,
            node_w_grad,
            gain_sum,
        ),
        "pix",
    )
    scaled = [grad_scale * entry for entry in summed]
    return (
        new_latents,
        grad_latents,
        scaled[0],
        scaled[1],
        scaled[2],
        scaled[3],
        scaled[4],
        scaled[5],
        scaled[6],
        scaled[7],
        scaled[8],
    )


def solution(mesh):
    return jax.shard_map(
        shards,
        mesh=mesh,
        in_specs=(
            P("pix", None),
            P(None, "lat"),
            P(None, "lat"),
            P("lat"),
            P("lat", None),
            P(None, "lat"),
            P(None, "lat"),
            P("lat"),
            P("lat", None),
            P(),
            P("pix"),
            P("pix"),
            P("pix"),
            P("pix"),
            P("pix", None, None),
            P("pix", None),
            P("pix", None),
        ),
        out_specs=(
            P("pix", None),
            P("pix", "lat"),
            P(None, "lat"),
            P(None, "lat"),
            P("lat"),
            P("lat", None),
            P(None, "lat"),
            P(None, "lat"),
            P("lat"),
            P("lat", None),
            P(),
        ),
        check_vma=False,
    )
```

profile of v0, /device:TPU:0, one launch (start us, length us, event | category | flops | bytes accessed | tf_op | source)
XLA Modules:
  0.0 465.5 jit_solution(5024926762899600851)
XLA Ops:
  8.9 3.0 collective-permute-start
  11.9 4.1 collective-permute-start.1
  16.6 1.7 gather_fusion
  18.3 38.1 %all-gather = bf16[128,512]{1,0:T(8,128)(2,1)S(1)} all-gather(bf16[8,512]{1,0:T(8,128)(2,1)S(1)} %gather_fusion), channel_id=2, replica_groups=mesh['pix'=16,'lat'=2] {'pix'}, dimensions={0}, use_global_device_ids=true | all-gather | bytes 139264 | tf_op jit(solution)/shard_map/all_gather | solution.py:78
  56.4 1.4 fusion.52
  57.8 1.1 fusion.53
  62.2 1.4 fusion.54
  63.6 1.2 fusion.51
  64.9 16.1 %gather_fusion.2 = f32[4096,256]{1,0:T(8,128)} fusion(f32[512,256]{1,0:T(8,128)S(1)} %fusion.54, s32[4096]{0:T(1024)S(1)} %broadcast_clamp_fusion), kind=kCustom, calls=%fused_computation.2 | custom fusion | bytes 8404992 | tf_op jit(solution)/shard_map/gather | solution.py:91
  81.3 16.6 %gather_fusion.1 = f32[4096,256]{1,0:T(8,128)} fusion(f32[896,256]{1,0:T(8,128)S(1)} %pad_maximum_fusion, s32[4096]{0:T(1024)S(1)} %broadcast_clamp_fusion.1), kind=kCustom, calls=%fused_computation.1 | custom fusion | bytes 8404992 | tf_op jit(solution)/shard_map/gather | solution.py:91
  97.9 4.9 %multiply_convert_fusion = bf16[4096,256]{1,0:T(8,128)(2,1)S(1)} fusion(f32[256]{0:T(256)S(1)} %copy-done.22, f32[4096,256]{1,0:T(8,128)} %gather_fusion.1, f32[4096,256]{1,0:T(8,128)} %gather_fusion.2), kind=kLoop, calls=%fused_computation.12 | loop fusion | flops 7340032 | bytes 10486784 | tf_op jit(solution)/shard_map/convert_element_type | solution.py:92
  102.9 1.3 fusion.55
  104.2 8.5 %fusion.11 = f32[32,128,512]{2,1,0:T(8,128)S(1)} fusion(f32[32,128,512]{2,1,0:T(8,128)S(1)} %bitcast.85, f32[32,128]{1,0:T(8,128)S(1)} %get-tuple-element.101, s32[32,128]{1,0:T(8,128)S(1)} %bitcast.94), kind=kOutput, calls=%fused_computation.21 | convolution fusion | flops 3222274048 | bytes 16809984 | tf_op jit(solution)/shard_map/ben,beh->bnh/dot_general | solution.py:28
  112.7 7.7 %fusion = f32[4,128,512]{2,0,1:T(4,128)S(1)} fusion(f32[32,128,512]{2,1,0:T(8,128)S(1)} %fusion.11, s32[32]{0:T(128)S(1)} %copy-done.20), kind=kOutput, calls=%fused_computation.5 | convolution fusion | flops 100663424 | bytes 9437312 | tf_op jit(solution)/shard_map/tb,bnh->tnh/dot_general | solution.py:36
  120.8 6.3 %all-reduce.10 = bf16[512,512]{1,0:T(8,128)(2,1)S(1)} all-reduce(f32[512,512]{1,0:T(8,128)S(1)} %bitcast.90), channel_id=1, replica_groups=mesh['pix'=16,'lat'=2] {'lat'}, use_global_device_ids=true, to_apply=%region_0.1 | all-reduce | flops 262144 | bytes 1572864 | tf_op jit(solution)/shard_map/psum | solution.py:95
  127.1 1.3 fusion.16
  129.2 2.2 fusion.45
  132.2 15.1 %all-reduce.7.cloned.1.call-done = f32[512,512]{1,0:T(8,128)} async-done(((f32[512,512]{1,0:T(8,128)}), f32[512,512]{1,0:T(8,128)}) %all-reduce.7.cloned.1.call-update) | async-done | bytes 1048592 | tf_op jit(solution)/shard_map/psum | solution.py:104
  147.3 1.5 reduce_sum.63
  148.8 1.5 multiply_reduce_fusion.2
  150.4 1.8 multiply_reduce_fusion
  152.2 1.3 multiply_convert_fusion.1
  153.8 1.2 fusion.44
  155.3 1.1 fusion.58
  156.5 1.3 fusion.56
  157.8 6.4 %all-reduce.11 = bf16[512,512]{1,0:T(8,128)(2,1)S(1)} all-reduce(f32[512,512]{1,0:T(8,128)S(1)} %fusion.57), channel_id=1, replica_groups=mesh['pix'=16,'lat'=2] {'lat'}, use_global_device_ids=true, to_apply=%region_6.7 | all-reduce | flops 262144 | bytes 1572864 | tf_op jit(solution)/shard_map/psum | solution.py:130
  164.2 17.5 %gather_fusion.3 = bf16[4096,512]{1,0:T(8,128)(2,1)} fusion(bf16[512,512]{1,0:T(8,128)(2,1)S(1)} %all-reduce.11, s32[4096]{0:T(1024)S(1)} %broadcast_clamp_fusion), kind=kCustom, calls=%fused_computation.3 | custom fusion | bytes 8404992 | tf_op jit(solution)/shard_map/gather | solution.py:132
  181.7 5.9 %fusion.50 = (f32[256]{0:T(256)S(1)}, f32[4096,256]{1,0:T(8,128)S(1)}) fusion(f32[256]{0:T(256)S(1)} %copy-done.22, f32[4096,256]{1,0:T(8,128)} %gather_fusion.1, f32[4096,256]{1,0:T(8,128)} %gather_fusion.2, bf16[256,512]{1,0:T(8,128)(2,1)S(1)} %copy-done, bf16[4096,512]{1,0:T(8,128)(2,1)} %gather_fusion.3, bf16[4096]{0:T(1024)(128)(2,1)S(1)} %get-tuple-element.100), kind=kOutput, calls=%fused_computation.107 | convolution fusion | flops 1087373056 | bytes 17049600 | tf_op jit(solution)/shard_map/dot_general | solution.py:134
  187.6 4.4 fusion.13
  192.0 2.7 fusion.14
  194.7 3.8 fusion.49
  198.8 5.5 %collective-permute-start.2 = (bf16[128,256]{1,0:T(8,128)(2,1)S(1)}, bf16[128,256]{1,0:T(8,128)(2,1)S(1)}, u32[]{:S(2)}, u32[]{:S(2)}) collective-permute-start(bf16[128,256]{1,0:T(8,128)(2,1)S(1)} %bitcast.97), channel_id=1, source_target_pairs={{2,0},{4,2},{6,4},{8,6},{10,8},{12,10},{14,12},{16,14},{18,16},{20... | collective-permute-start | bytes 196616 | tf_op jit(solution)/shard_map/ppermute | solution.py:13
  205.5 5.8 %fusion.17 = bf16[4,128,256]{2,0,1:T(4,128)(2,1)S(1)} fusion(f32[32,128,256]{2,1,0:T(8,128)} %fusion.13, s32[32]{0:T(128)S(1)} %copy-done.20), kind=kOutput, calls=%fused_computation.35 | convolution fusion | flops 50462848 | bytes 4456576 | tf_op jit(solution)/shard_map/tb,bnh->tnh/dot_general | solution.py:36
  212.0 1.1 convolution_bitcast_fusion.1
  214.1 1.9 broadcast_select_fusion
  215.9 4.1 scatter-add.12
  220.0 1.1 copy.56
  221.2 61.4 %reduce-scatter.3.cloned.1.call-done = f32[8,256]{1,0:T(8,128)} async-done(((f32[128,256]{1,0:T(8,128)}), f32[8,256]{1,0:T(8,128)}) %reduce-scatter.3.cloned.1.call-update) | async-done | bytes 8208 | tf_op jit(solution)/shard_map/reduce_scatter | solution.py:147
  283.6 1.6 convolution_add_fusion.1
  285.2 2.2 fusion.15
  287.5 2.1 convolution_bitcast_fusion
  289.5 4.5 fusion.6
  294.0 1.1 convolution_bitcast_fusion.2
  295.3 38.9 %all-reduce = (f32[256]{0:T(256)S(1)}, f32[256]{0:T(256)S(1)}, f32[512]{0:T(512)S(1)}) all-reduce(f32[256]{0:T(256)S(1)} %get-tuple-element.105, f32[256]{0:T(256)S(1)} %get-tuple-element.92, f32[512]{0:T(512)S(1)} %get-tuple-element.78), channel_id=1, replica_groups=mesh['pix'=16,'lat'=2] {'pix'}, use_global_device_ids=true, to_apply=%region_14.15 | all-reduce | flops 1024 | bytes 8192 | tf_op jit(solution)/shard_map/psum | solution.py:166
  335.9 1.8 dynamic-slice_add_fusion
  337.8 112.8 %all-reduce.9.cloned.1.call-done = (f32[512,256]{0,1:T(8,128)}, f32[512,256]{0,1:T(8,128)}, f32[256,512]{1,0:T(8,128)}, f32[512,256]{0,1:T(8,128)}, f32[512,256]{0,1:T(8,128)}, /*index=5*/f32[256,512]{1,0:T(8,128)}) async-done(((f32[512,256]{0,1:T(8,128)}, f32[512,256]{0,1:T(8,128)}, f32[256,512]{1,0:T(8,128)}, f32[512,256]{0,1:T(8,128)}, f32[512,256]{0,1:T(8,128)}, /*index=5*/f32[256,512]{1,0:T(8,128)}), ...) | async-done | bytes 3145744 | tf_op jit(solution)/shard_map/psum | solution.py:166
  450.6 1.2 broadcast_multiply_fusion.5
  452.8 1.1 broadcast_multiply_fusion.4
  (108 shorter events, 19.7 us)
Async XLA Ops:
  7.2 95.7 %copy-start = (bf16[256,512]{1,0:T(8,128)(2,1)S(1)}, bf16[256,512]{1,0:T(8,128)(2,1)}, u32[]{:S(2)}) copy-start(bf16[256,512]{1,0:T(8,128)(2,1)} %param.23) | copy-start | bytes 786436
  7.2 56.4 %copy-start.1 = (bf16[512,512]{1,0:T(8,128)(2,1)S(1)}, bf16[512,512]{1,0:T(8,128)(2,1)}, u32[]{:S(2)}) copy-start(bf16[512,512]{1,0:T(8,128)(2,1)} %param.19) | copy-start | bytes 1572868
  7.2 140.1 %all-reduce.7.cloned.1.call-start = ((), (), s32[]{:S(2)}) async-start(), calls=%async_computation.2 | async-start | bytes 2097152 | tf_op jit(solution)/shard_map/psum | solution.py:104
  8.9 72.1 %collective-permute-start = (bf16[128,512]{1,0:T(8,128)(2,1)S(1)}, bf16[128,512]{1,0:T(8,128)(2,1)S(1)}, u32[]{:S(2)}, u32[]{:S(2)}) collective-permute-start(bf16[128,512]{1,0:T(8,128)(2,1)S(1)} %dynamic-slice_bitcast_fusion), channel_id=1, source_target_pairs={{30,0},{0,2},{2,4},{4,6},{6,8},{8,10},{10,12},{12,14},{14,16},{16,... | collective-permute-start | bytes 393224 | tf_op jit(solution)/shard_map/ppermute | solution.py:13
  11.9 69.1 %collective-permute-start.1 = (bf16[128,512]{1,0:T(8,128)(2,1)S(1)}, bf16[128,512]{1,0:T(8,128)(2,1)S(1)}, u32[]{:S(2)}, u32[]{:S(2)}) collective-permute-start(bf16[128,512]{1,0:T(8,128)(2,1)S(1)} %dynamic-slice_bitcast_fusion), channel_id=1, source_target_pairs={{2,0},{4,2},{6,4},{8,6},{10,8},{12,10},{14,12},{16,14},{18,16},{20... | collective-permute-start | bytes 393224 | tf_op jit(solution)/shard_map/ppermute | solution.py:13
  64.9 16.1 %copy-start.18 = (s32[32,128]{1,0:T(8,128)S(1)}, s32[32,128]{1,0:T(8,128)}, u32[]{:S(2)}) copy-start(s32[32,128]{1,0:T(8,128)} %param.34) | copy-start | bytes 49156
  64.9 16.1 %copy-start.8 = (bf16[512,256]{1,0:T(8,128)(2,1)S(1)}, bf16[512,256]{1,0:T(8,128)(2,1)}, u32[]{:S(2)}) copy-start(bf16[512,256]{1,0:T(8,128)(2,1)} %param.20) | copy-start | bytes 786436
  81.3 16.6 %copy-start.22 = (f32[256]{0:T(256)S(1)}, f32[256]{0:T(256)}, u32[]{:S(2)}) copy-start(f32[256]{0:T(256)} %param.22) | copy-start | bytes 3076
  102.8 1.3 copy-start.3
  104.2 8.5 %copy-start.20 = (s32[32]{0:T(128)S(1)}, s32[32]{0:T(128)}, u32[]{:S(2)}) copy-start(s32[32]{0:T(128)} %param.31) | copy-start | bytes 388
  112.7 14.3 %copy-start.21 = (f32[256]{0:T(256)S(1)}, f32[256]{0:T(256)}, u32[]{:S(2)}) copy-start(f32[256]{0:T(256)} %param.26) | copy-start | bytes 3076
  120.4 11.1 %copy-start.24 = (s32[3]{0:T(128)S(1)}, s32[3]{0:T(128)}, u32[]{:S(2)}) copy-start(s32[3]{0:T(128)} %constant.62.clone.1) | copy-start | bytes 40
  127.1 23.3 %copy-start.5 = (bf16[512,512]{1,0:T(8,128)(2,1)S(1)}, bf16[512,512]{1,0:T(8,128)(2,1)}, u32[]{:S(2)}) copy-start(bf16[512,512]{1,0:T(8,128)(2,1)} %param.35) | copy-start | bytes 1572868
  127.1 23.3 %copy-start.19 = (f32[512]{0:T(512)S(1)}, f32[512]{0:T(512)}, u32[]{:S(2)}) copy-start(f32[512]{0:T(512)} %param.28) | copy-start | bytes 6148
  128.4 0.8 copy-start.12
  131.4 22.0 %copy-start.13 = (f32[512,256]{1,0:T(8,128)S(1)}, f32[512,256]{1,0:T(8,128)}, u32[]{:S(2)}) copy-start(f32[512,256]{1,0:T(8,128)} %copy-done.12) | copy-start | bytes 1572868
  131.5 151.1 %reduce-scatter.3.cloned.1.call-start = ((), (), s32[]{:S(2)}) async-start(), calls=%async_computation.3 | async-start | bytes 139264 | tf_op jit(solution)/shard_map/reduce_scatter | solution.py:147
  147.3 4.8 %copy-start.2 = (f32[512,512]{1,0:T(8,128)S(1)}, f32[512,512]{1,0:T(8,128)}, u32[]{:S(2)}) copy-start(f32[512,512]{1,0:T(8,128)} %all-reduce.7.cloned.1.call-done) | copy-start | bytes 3145732
  148.8 4.7 copy-start.25
  153.4 1.6 copy-start.10
  153.4 3.0 copy-start.11
  153.8 2.7 copy-start.7
  192.0 2.7 copy-start.23
  198.8 15.3 %collective-permute-start.2 = (bf16[128,256]{1,0:T(8,128)(2,1)S(1)}, bf16[128,256]{1,0:T(8,128)(2,1)S(1)}, u32[]{:S(2)}, u32[]{:S(2)}) collective-permute-start(bf16[128,256]{1,0:T(8,128)(2,1)S(1)} %bitcast.97), channel_id=1, source_target_pairs={{2,0},{4,2},{6,4},{8,6},{10,8},{12,10},{14,12},{16,14},{18,16},{20... | collective-permute-start | bytes 196616 | tf_op jit(solution)/shard_map/ppermute | solution.py:13
  204.3 9.7 %collective-permute-start.3 = (bf16[128,256]{1,0:T(8,128)(2,1)S(1)}, bf16[128,256]{1,0:T(8,128)(2,1)S(1)}, u32[]{:S(2)}, u32[]{:S(2)}) collective-permute-start(bf16[128,256]{1,0:T(8,128)(2,1)S(1)} %bitcast.98), channel_id=1, source_target_pairs={{30,0},{0,2},{2,4},{4,6},{6,8},{8,10},{10,12},{12,14},{14,16},{16,... | collective-permute-start | bytes 196616 | tf_op jit(solution)/shard_map/ppermute | solution.py:13
  205.2 130.8 %reduce-scatter.5.cloned.1.call-start = ((), (), s32[]{:S(2)}) async-start(), calls=%async_computation.4 | async-start | bytes 786432 | tf_op jit(solution)/shard_map/reduce_scatter | solution.py:160
  211.3 0.7 copy-start.9
  215.9 73.6 %copy-start.4 = (bf16[4096,256]{1,0:T(8,128)(2,1)S(1)}, bf16[4096,256]{1,0:T(8,128)(2,1)}, u32[]{:S(2)}) copy-start(bf16[4096,256]{1,0:T(8,128)(2,1)} %copy-done.3) | copy-start | bytes 6291460
  287.4 163.2 %all-reduce.9.cloned.1.call-start = ((), (), s32[]{:S(2)}) async-start(), calls=%async_computation.5 | async-start | bytes 6291456 | tf_op jit(solution)/shard_map/psum | solution.py:166
  294.0 1.2 copy-start.6
  450.6 4.3 copy-start.17
  450.6 5.4 %copy-start.16 = (f32[512,256]{0,1:T(8,128)S(1)}, f32[512,256]{0,1:T(8,128)}, u32[]{:S(2)}) copy-start(f32[512,256]{0,1:T(8,128)} %get-tuple-element.88) | copy-start | bytes 1572868
  450.6 6.4 %copy-start.15 = (f32[256,512]{1,0:T(8,128)S(1)}, f32[256,512]{1,0:T(8,128)}, u32[]{:S(2)}) copy-start(f32[256,512]{1,0:T(8,128)} %get-tuple-element.89) | copy-start | bytes 1572868
  451.8 6.1 %copy-start.14 = (f32[256,512]{1,0:T(8,128)S(1)}, f32[256,512]{1,0:T(8,128)}, u32[]{:S(2)}) copy-start(f32[256,512]{1,0:T(8,128)} %get-tuple-element.86) | copy-start | bytes 1572868
Sparse Core Ops, SparseCore 0:
  131.6 15.7 all-reduce.6
  205.3 77.1 reduce-scatter.2
  287.5 4.2 reduce-scatter.4
  299.8 150.6 all-reduce.8
where the time goes:
time: 469 us; the launch traced here: 465 us
  waiting for transfers between devices  189 us (40%)
  blocking collectives  89.7 us (19%)
  local copies, waits for them, and re-layouts  67 us (14%)
  matrix products  65.9 us (14%)
  other arithmetic  25.2 us (5%)
  between operations  15.3 us (3%)
  starting transfers between devices  13 us (3%)
    psum x1, waiting for transfers between devices, shards(): lax.psum((send_w_grad, recv_w_grad, edge_bias_sum, msg_w_grad, self_w_gra...  113 us
    reduce_scatter x1, waiting for transfers between devices, shards(): lax.psum_scatter(panel_part, 'pix', scatter_dimension=0, tiled=True)  61.4 us
    psum x1, blocking collectives, shards(): lax.psum((send_w_grad, recv_w_grad, edge_bias_sum, msg_w_grad, self_w_gra...  38.9 us
    all_gather x1, blocking collectives, shards(): lax.all_gather(latents[coarse_ids], 'pix', axis=0, tiled=True)  38.1 us
    gather x2, local copies, waits for them, and re-layouts, shards(): edge_pre = source_proj[senders] + recv_proj[receivers] + edge_bias  32.7 us
    gather x1, local copies, waits for them, and re-layouts, shards(): msg_cot = agg_cot_bf[receivers] * edge_weight.astype(jnp.bfloat16)[:, None]  17.5 us
    dot_general x3, matrix products, tile_sums(): jnp.einsum('tb,bnh->tnh', selector, per_block, precision=lax.Precision.HI...  17.3 us
    dot_general x3, matrix products, tile_sums(): jnp.einsum('ben,beh->bnh', incidence, values.reshape(block_count, tile_le...  15.6 us
  transfers between devices with their start and end apart: 8, of which 3 were waited for; matrix products, arithmetic and copies ran while one was open for 12% of the time, Pallas kernels for 0%

commit v1 on v0

--- a/solution.py
+++ b/solution.py
@@ -1,10 +1,38 @@
+import functools
 import math
 import jax
 import jax.numpy as jnp
 from jax import lax
 from jax.sharding import PartitionSpec as P
+from jax.lax import axis_index, axis_size, ppermute
 
 norm_eps = 1e-05
+
+
+def _fit_blocks(patch, group_axis):
+    z_new = axis_size(group_axis)
+    parts_out = axis_index(group_axis)
+    earlier, reply, taken_in = (z_new, parts_out, patch.shape[0])
+    inbox = tuple(((dev, (dev + 1) % earlier) for dev in range(earlier)))
+    column = tuple(((dev, (dev - 1) % earlier) for dev in range(earlier)))
+    latest = jnp.zeros((*patch.shape[:0], earlier * taken_in, *patch.shape[1:]), patch.dtype)
+    latest = lax.dynamic_update_slice_in_dim(latest, patch, reply * taken_in, axis=0)
+    extra = work_now = patch
+    local_now = earlier // 2
+    for nth in [*range(1, local_now + 1)]:
+        extra = ppermute(extra, axis_name=group_axis, perm=inbox)
+        latest = lax.dynamic_update_slice_in_dim(
+            latest, extra, (reply - nth) % earlier * taken_in, axis=0
+        )
+        if nth < earlier - local_now:
+            work_now = ppermute(work_now, perm=column, axis_name=group_axis)
+            latest = lax.dynamic_update_slice_in_dim(
+                latest, work_now, (reply + nth) % earlier * taken_in, axis=0
+            )
+    return latest
+
+
+_fill_domain = functools.partial(_fit_blocks, group_axis="pix")
 
 
 def from_behind(block, axis, distance):
@@ -75,9 +103,7 @@
         jnp.concatenate([from_left, from_right], axis=0), w_send, preferred_element_type=jnp.float32
     )
     panel_proj = jnp.dot(
-        lax.all_gather(latents[coarse_ids], "pix", axis=0, tiled=True),
-        w_send,
-        preferred_element_type=jnp.float32,
+        _fill_domain(latents[coarse_ids]), w_send, preferred_element_type=jnp.float32
     )
     source_proj = jnp.concatenate([send_proj, side_proj, panel_proj], axis=0)
     source_tiles = source_proj.shape[0] // tile_len

time: 469 us -> 487 us (1.038)
  starting transfers between devices: 13 us -> 52.4 us
  blocking collectives: 89.7 us -> 51.5 us
  waiting for transfers between devices: 189 us -> 206 us
    ppermute x0 -> x15, starting transfers between devices: none -> 40.8 us  [the longest x7 37.8 us: _fit_blocks(): work_now = ppermute(work_now, perm=column, axis_name=group_axis)]
    all_gather x1 -> x0, blocking collectives: 38.1 us -> none  [shards(): lax.all_gather(latents[coarse_ids], 'pix', axis=0, tiled=True)]
    ppermute x0 -> x15, waiting for transfers between devices: none -> 16.9 us  [the longest x8 16.9 us: _fit_blocks(): extra = ppermute(extra, axis_name=group_axis, perm=inbox)]
  transfers between devices with their start and end apart: 8 -> 23, of which waited for: 3 -> 10; matrix products, arithmetic and copies ran while one was open for 12% -> 11% of each run, Pallas kernels for 0% -> 0%
where the time goes in v1:
time: 487 us; the launch traced here: 482 us
  waiting for transfers between devices  206 us (42%)
  local copies, waits for them, and re-layouts  66.4 us (14%)
  matrix products  64.4 us (13%)
  starting transfers between devices  52.4 us (11%)
  blocking collectives  51.5 us (11%)
  other arithmetic  26 us (5%)
  between operations  15.4 us (3%)
    psum x1, waiting for transfers between devices, shards(): lax.psum((send_w_grad, recv_w_grad, edge_bias_sum, msg_w_grad, self_w_gra...  113 us
    reduce_scatter x1, waiting for transfers between devices, shards(): lax.psum_scatter(panel_part, 'pix', scatter_dimension=0, tiled=True)  61.5 us
    psum x1, blocking collectives, shards(): lax.psum((send_w_grad, recv_w_grad, edge_bias_sum, msg_w_grad, self_w_gra...  38.9 us
    ppermute x7, starting transfers between devices, _fit_blocks(): work_now = ppermute(work_now, perm=column, axis_name=group_axis)  37.8 us
    gather x2, local copies, waits for them, and re-layouts, shards(): edge_pre = source_proj[senders] + recv_proj[receivers] + edge_bias  32.5 us
    gather x1, local copies, waits for them, and re-layouts, shards(): msg_cot = agg_cot_bf[receivers] * edge_weight.astype(jnp.bfloat16)[:, None]  17.8 us
    dot_general x3, matrix products, tile_sums(): jnp.einsum('tb,bnh->tnh', selector, per_block, precision=lax.Precision.HI...  17.3 us
    ppermute x8, waiting for transfers between devices, _fit_blocks(): extra = ppermute(extra, axis_name=group_axis, perm=inbox)  16.9 us
  transfers between devices with their start and end apart: 23, of which 10 were waited for; matrix products, arithmetic and copies ran while one was open for 11% of the time, Pallas kernels for 0%

profile of v1, /device:TPU:0, one launch (start us, length us, event | category | flops | bytes accessed | tf_op | source)
XLA Modules:
  0.0 482.5 jit_solution(457700939713317495)
XLA Ops:
  7.9 1.7 gather_fusion
  9.6 3.0 collective-permute-start.2
  12.6 4.1 collective-permute-start.3
  18.3 5.6 %collective-permute-start.1 = (bf16[128,512]{1,0:T(8,128)(2,1)S(1)}, bf16[128,512]{1,0:T(8,128)(2,1)S(1)}, u32[]{:S(2)}, u32[]{:S(2)}) collective-permute-start(bf16[128,512]{1,0:T(8,128)(2,1)S(1)} %dynamic-slice_bitcast_fusion), channel_id=1, source_target_pairs={{2,0},{4,2},{6,4},{8,6},{10,8},{12,10},{14,12},{16,14},{18,16},{20... | collective-permute-start | bytes 393224 | tf_op jit(solution)/shard_map/ppermute | solution.py:41
  28.6 1.4 fusion.54
  30.7 1.4 fusion.51
  32.4 16.2 %gather_fusion.2 = f32[4096,256]{1,0:T(8,128)} fusion(f32[512,256]{1,0:T(8,128)S(1)} %fusion.54, s32[4096]{0:T(1024)S(1)} %broadcast_clamp_fusion), kind=kCustom, calls=%fused_computation.2 | custom fusion | bytes 8404992 | tf_op jit(solution)/shard_map/gather | solution.py:117
  48.6 5.6 %collective-permute-start.5 = (bf16[8,512]{1,0:T(8,128)(2,1)S(1)}, bf16[8,512]{1,0:T(8,128)(2,1)S(1)}, u32[]{:S(2)}, u32[]{:S(2)}) collective-permute-start(bf16[8,512]{1,0:T(8,128)(2,1)S(1)} %collective-permute-done.3), channel_id=1, source_target_pairs={{0,30},{2,0},{4,2},{6,4},{8,6},{10,8},{12,10},{14,12},{16,14},{18,... | collective-permute-start | bytes 24584 | tf_op jit(solution)/shard_map/ppermute | solution.py:28
  54.2 1.6 collective-permute-done.4
  55.9 5.6 %collective-permute-start.7 = (bf16[8,512]{1,0:T(8,128)(2,1)S(1)}, bf16[8,512]{1,0:T(8,128)(2,1)S(1)}, u32[]{:S(2)}, u32[]{:S(2)}) collective-permute-start(bf16[8,512]{1,0:T(8,128)(2,1)S(1)} %collective-permute-done.5), channel_id=1, source_target_pairs={{0,30},{2,0},{4,2},{6,4},{8,6},{10,8},{12,10},{14,12},{16,14},{18,... | collective-permute-start | bytes 24584 | tf_op jit(solution)/shard_map/ppermute | solution.py:28
  61.5 1.6 collective-permute-done.6
  63.1 5.6 %collective-permute-start.9 = (bf16[8,512]{1,0:T(8,128)(2,1)S(1)}, bf16[8,512]{1,0:T(8,128)(2,1)S(1)}, u32[]{:S(2)}, u32[]{:S(2)}) collective-permute-start(bf16[8,512]{1,0:T(8,128)(2,1)S(1)} %collective-permute-done.7), channel_id=1, source_target_pairs={{0,30},{2,0},{4,2},{6,4},{8,6},{10,8},{12,10},{14,12},{16,14},{18,... | collective-permute-start | bytes 24584 | tf_op jit(solution)/shard_map/ppermute | solution.py:28
  68.7 1.6 collective-permute-done.8
  70.4 5.6 %collective-permute-start.11 = (bf16[8,512]{1,0:T(8,128)(2,1)S(1)}, bf16[8,512]{1,0:T(8,128)(2,1)S(1)}, u32[]{:S(2)}, u32[]{:S(2)}) collective-permute-start(bf16[8,512]{1,0:T(8,128)(2,1)S(1)} %collective-permute-done.9), channel_id=1, source_target_pairs={{0,30},{2,0},{4,2},{6,4},{8,6},{10,8},{12,10},{14,12},{16,14},{18,... | collective-permute-start | bytes 24584 | tf_op jit(solution)/shard_map/ppermute | solution.py:28
  76.0 1.6 collective-permute-done.10
  77.6 5.6 %collective-permute-start.13 = (bf16[8,512]{1,0:T(8,128)(2,1)S(1)}, bf16[8,512]{1,0:T(8,128)(2,1)S(1)}, u32[]{:S(2)}, u32[]{:S(2)}) collective-permute-start(bf16[8,512]{1,0:T(8,128)(2,1)S(1)} %collective-permute-done.11), channel_id=1, source_target_pairs={{0,30},{2,0},{4,2},{6,4},{8,6},{10,8},{12,10},{14,12},{16,14},{18,... | collective-permute-start | bytes 24584 | tf_op jit(solution)/shard_map/ppermute | solution.py:28
  83.2 1.6 collective-permute-done.12
  84.9 5.6 %collective-permute-start.15 = (bf16[8,512]{1,0:T(8,128)(2,1)S(1)}, bf16[8,512]{1,0:T(8,128)(2,1)S(1)}, u32[]{:S(2)}, u32[]{:S(2)}) collective-permute-start(bf16[8,512]{1,0:T(8,128)(2,1)S(1)} %collective-permute-done.13), channel_id=1, source_target_pairs={{0,30},{2,0},{4,2},{6,4},{8,6},{10,8},{12,10},{14,12},{16,14},{18,... | collective-permute-start | bytes 24584 | tf_op jit(solution)/shard_map/ppermute | solution.py:28
  90.5 1.6 collective-permute-done.14
  92.1 7.2 %collective-permute-done.16 = bf16[8,512]{1,0:T(8,128)(2,1)S(1)} collective-permute-done((bf16[8,512]{1,0:T(8,128)(2,1)S(1)}, bf16[8,512]{1,0:T(8,128)(2,1)S(1)}, u32[]{:S(2)}, u32[]{:S(2)}) %collective-permute-start.16) | collective-permute-done | bytes 8224 | tf_op jit(solution)/shard_map/ppermute | solution.py:23
  99.9 16.3 %gather_fusion.1 = f32[4096,256]{1,0:T(8,128)} fusion(f32[896,256]{1,0:T(8,128)S(1)} %pad_maximum_fusion, s32[4096]{0:T(1024)S(1)} %broadcast_clamp_fusion.1), kind=kCustom, calls=%fused_computation.1 | custom fusion | bytes 8404992 | tf_op jit(solution)/shard_map/gather | solution.py:117
  116.2 4.9 %multiply_convert_fusion = bf16[4096,256]{1,0:T(8,128)(2,1)S(1)} fusion(f32[256]{0:T(256)S(1)} %copy-done.22, f32[4096,256]{1,0:T(8,128)} %gather_fusion.1, f32[4096,256]{1,0:T(8,128)} %gather_fusion.2), kind=kLoop, calls=%fused_computation.12 | loop fusion | flops 7340032 | bytes 10486784 | tf_op jit(solution)/shard_map/convert_element_type | solution.py:118
  122.4 8.5 %fusion.11 = f32[32,128,512]{2,1,0:T(8,128)S(1)} fusion(f32[32,128,512]{2,1,0:T(8,128)S(1)} %bitcast.85, f32[32,128]{1,0:T(8,128)S(1)} %get-tuple-element.101, s32[32,128]{1,0:T(8,128)S(1)} %bitcast.94), kind=kOutput, calls=%fused_computation.21 | convolution fusion | flops 3222274048 | bytes 16809984 | tf_op jit(solution)/shard_map/ben,beh->bnh/dot_general | solution.py:56
  131.0 7.7 %fusion = f32[4,128,512]{2,0,1:T(4,128)S(1)} fusion(f32[32,128,512]{2,1,0:T(8,128)S(1)} %fusion.11, s32[32]{0:T(128)S(1)} %copy-done.20), kind=kOutput, calls=%fused_computation.5 | convolution fusion | flops 100663424 | bytes 9437312 | tf_op jit(solution)/shard_map/tb,bnh->tnh/dot_general | solution.py:64
  139.1 6.3 %all-reduce.10 = bf16[512,512]{1,0:T(8,128)(2,1)S(1)} all-reduce(f32[512,512]{1,0:T(8,128)S(1)} %bitcast.90), channel_id=1, replica_groups=mesh['pix'=16,'lat'=2] {'lat'}, use_global_device_ids=true, to_apply=%region_0.1 | all-reduce | flops 262144 | bytes 1572864 | tf_op jit(solution)/shard_map/psum | solution.py:121
  145.7 2.5 fusion.45
  149.0 15.1 %all-reduce.7.cloned.1.call-done = f32[512,512]{1,0:T(8,128)} async-done(((f32[512,512]{1,0:T(8,128)}), f32[512,512]{1,0:T(8,128)}) %all-reduce.7.cloned.1.call-update) | async-done | bytes 1048592 | tf_op jit(solution)/shard_map/psum | solution.py:130
  164.1 1.5 reduce_sum.63
  165.6 1.5 multiply_reduce_fusion.2
  167.2 1.8 multiply_reduce_fusion
  174.6 6.3 %all-reduce.11 = bf16[512,512]{1,0:T(8,128)(2,1)S(1)} all-reduce(f32[512,512]{1,0:T(8,128)S(1)} %fusion.57), channel_id=1, replica_groups=mesh['pix'=16,'lat'=2] {'lat'}, use_global_device_ids=true, to_apply=%region_6.7 | all-reduce | flops 262144 | bytes 1572864 | tf_op jit(solution)/shard_map/psum | solution.py:156
  181.0 17.8 %gather_fusion.3 = bf16[4096,512]{1,0:T(8,128)(2,1)} fusion(bf16[512,512]{1,0:T(8,128)(2,1)S(1)} %all-reduce.11, s32[4096]{0:T(1024)S(1)} %broadcast_clamp_fusion), kind=kCustom, calls=%fused_computation.3 | custom fusion | bytes 8404992 | tf_op jit(solution)/shard_map/gather | solution.py:158
  198.7 5.9 %fusion.50 = (f32[256]{0:T(256)S(1)}, f32[4096,256]{1,0:T(8,128)S(1)}) fusion(f32[256]{0:T(256)S(1)} %copy-done.22, f32[4096,256]{1,0:T(8,128)} %gather_fusion.1, f32[4096,256]{1,0:T(8,128)} %gather_fusion.2, bf16[256,512]{1,0:T(8,128)(2,1)S(1)} %copy-done, bf16[4096,512]{1,0:T(8,128)(2,1)} %gather_fusion.3, bf16[4096]{0:T(1024)(128)(2,1)S(1)} %get-tuple-element.100), kind=kOutput, calls=%fused_computation.123 | convolution fusion | flops 1087373056 | bytes 17049600 | tf_op jit(solution)/shard_map/dot_general | solution.py:160
  204.7 4.4 fusion.13
  209.1 2.7 fusion.14
  211.7 3.8 fusion.49
  215.8 5.5 %collective-permute-start.17 = (bf16[128,256]{1,0:T(8,128)(2,1)S(1)}, bf16[128,256]{1,0:T(8,128)(2,1)S(1)}, u32[]{:S(2)}, u32[]{:S(2)}) collective-permute-start(bf16[128,256]{1,0:T(8,128)(2,1)S(1)} %bitcast.97), channel_id=1, source_target_pairs={{2,0},{4,2},{6,4},{8,6},{10,8},{12,10},{14,12},{16,14},{18,16},{20... | collective-permute-start | bytes 196616 | tf_op jit(solution)/shard_map/ppermute | solution.py:41
  222.5 5.8 %fusion.17 = bf16[4,128,256]{2,0,1:T(4,128)(2,1)S(1)} fusion(f32[32,128,256]{2,1,0:T(8,128)} %fusion.13, s32[32]{0:T(128)S(1)} %copy-done.20), kind=kOutput, calls=%fused_computation.35 | convolution fusion | flops 50462848 | bytes 4456576 | tf_op jit(solution)/shard_map/tb,bnh->tnh/dot_general | solution.py:64
  231.1 1.9 broadcast_select_fusion
  232.9 4.1 scatter-add.12
  238.1 61.5 %reduce-scatter.3.cloned.1.call-done = f32[8,256]{1,0:T(8,128)} async-done(((f32[128,256]{1,0:T(8,128)}), f32[8,256]{1,0:T(8,128)}) %reduce-scatter.3.cloned.1.call-update) | async-done | bytes 8208 | tf_op jit(solution)/shard_map/reduce_scatter | solution.py:173
  300.7 1.6 convolution_add_fusion.1
  302.3 2.2 fusion.15
  304.5 2.1 convolution_bitcast_fusion
  306.6 4.5 fusion.6
  312.4 38.9 %all-reduce = (f32[256]{0:T(256)S(1)}, f32[256]{0:T(256)S(1)}, f32[512]{0:T(512)S(1)}) all-reduce(f32[256]{0:T(256)S(1)} %get-tuple-element.105, f32[256]{0:T(256)S(1)} %get-tuple-element.92, f32[512]{0:T(512)S(1)} %get-tuple-element.78), channel_id=1, replica_groups=mesh['pix'=16,'lat'=2] {'pix'}, use_global_device_ids=true, to_apply=%region_14.15 | all-reduce | flops 1024 | bytes 8192 | tf_op jit(solution)/shard_map/psum | solution.py:192
  353.0 1.8 dynamic-slice_add_fusion
  354.8 112.8 %all-reduce.9.cloned.1.call-done = (f32[512,256]{0,1:T(8,128)}, f32[512,256]{0,1:T(8,128)}, f32[256,512]{1,0:T(8,128)}, f32[512,256]{0,1:T(8,128)}, f32[512,256]{0,1:T(8,128)}, /*index=5*/f32[256,512]{1,0:T(8,128)}) async-done(((f32[512,256]{0,1:T(8,128)}, f32[512,256]{0,1:T(8,128)}, f32[256,512]{1,0:T(8,128)}, f32[512,256]{0,1:T(8,128)}, f32[512,256]{0,1:T(8,128)}, /*index=5*/f32[256,512]{1,0:T(8,128)}), ...) | async-done | bytes 3145744 | tf_op jit(solution)/shard_map/psum | solution.py:192
  (154 shorter events, 33.4 us)
Async XLA Ops:
  7.2 113.9 %copy-start = (bf16[256,512]{1,0:T(8,128)(2,1)S(1)}, bf16[256,512]{1,0:T(8,128)(2,1)}, u32[]{:S(2)}) copy-start(bf16[256,512]{1,0:T(8,128)(2,1)} %param.23) | copy-start | bytes 786436
  7.2 156.9 %all-reduce.7.cloned.1.call-start = ((), (), s32[]{:S(2)}) async-start(), calls=%async_computation.2 | async-start | bytes 2097152 | tf_op jit(solution)/shard_map/psum | solution.py:130
  9.6 39.0 %collective-permute-start.2 = (bf16[8,512]{1,0:T(8,128)(2,1)S(1)}, bf16[8,512]{1,0:T(8,128)(2,1)S(1)}, u32[]{:S(2)}, u32[]{:S(2)}) collective-permute-start(bf16[8,512]{1,0:T(8,128)(2,1)S(1)} %gather_fusion), channel_id=1, source_target_pairs={{0,2},{2,4},{4,6},{6,8},{8,10},{10,12},{12,14},{14,16},{16,18},{18... | collective-permute-start | bytes 24584 | tf_op jit(solution)/shard_map/ppermute | solution.py:23
  12.6 36.0 %collective-permute-start.3 = (bf16[8,512]{1,0:T(8,128)(2,1)S(1)}, bf16[8,512]{1,0:T(8,128)(2,1)S(1)}, u32[]{:S(2)}, u32[]{:S(2)}) collective-permute-start(bf16[8,512]{1,0:T(8,128)(2,1)S(1)} %gather_fusion), channel_id=1, source_target_pairs={{0,30},{2,0},{4,2},{6,4},{8,6},{10,8},{12,10},{14,12},{16,14},{18,... | collective-permute-start | bytes 24584 | tf_op jit(solution)/shard_map/ppermute | solution.py:28
  18.2 81.3 %collective-permute-start = (bf16[128,512]{1,0:T(8,128)(2,1)S(1)}, bf16[128,512]{1,0:T(8,128)(2,1)S(1)}, u32[]{:S(2)}, u32[]{:S(2)}) collective-permute-start(bf16[128,512]{1,0:T(8,128)(2,1)S(1)} %dynamic-slice_bitcast_fusion), channel_id=1, source_target_pairs={{30,0},{0,2},{2,4},{4,6},{6,8},{8,10},{10,12},{12,14},{14,16},{16,... | collective-permute-start | bytes 393224 | tf_op jit(solution)/shard_map/ppermute | solution.py:41
  18.3 81.3 %collective-permute-start.1 = (bf16[128,512]{1,0:T(8,128)(2,1)S(1)}, bf16[128,512]{1,0:T(8,128)(2,1)S(1)}, u32[]{:S(2)}, u32[]{:S(2)}) collective-permute-start(bf16[128,512]{1,0:T(8,128)(2,1)S(1)} %dynamic-slice_bitcast_fusion), channel_id=1, source_target_pairs={{2,0},{4,2},{6,4},{8,6},{10,8},{12,10},{14,12},{16,14},{18,16},{20... | collective-permute-start | bytes 393224 | tf_op jit(solution)/shard_map/ppermute | solution.py:41
  32.4 67.0 %copy-start.8 = (bf16[512,256]{1,0:T(8,128)(2,1)S(1)}, bf16[512,256]{1,0:T(8,128)(2,1)}, u32[]{:S(2)}) copy-start(bf16[512,256]{1,0:T(8,128)(2,1)} %param.20) | copy-start | bytes 786436
  48.6 7.2 %collective-permute-start.4 = (bf16[8,512]{1,0:T(8,128)(2,1)S(1)}, bf16[8,512]{1,0:T(8,128)(2,1)S(1)}, u32[]{:S(2)}, u32[]{:S(2)}) collective-permute-start(bf16[8,512]{1,0:T(8,128)(2,1)S(1)} %collective-permute-done.2), channel_id=1, source_target_pairs={{0,2},{2,4},{4,6},{6,8},{8,10},{10,12},{12,14},{14,16},{16,18},{18... | collective-permute-start | bytes 24584 | tf_op jit(solution)/shard_map/ppermute | solution.py:23
  48.6 7.2 %collective-permute-start.5 = (bf16[8,512]{1,0:T(8,128)(2,1)S(1)}, bf16[8,512]{1,0:T(8,128)(2,1)S(1)}, u32[]{:S(2)}, u32[]{:S(2)}) collective-permute-start(bf16[8,512]{1,0:T(8,128)(2,1)S(1)} %collective-permute-done.3), channel_id=1, source_target_pairs={{0,30},{2,0},{4,2},{6,4},{8,6},{10,8},{12,10},{14,12},{16,14},{18,... | collective-permute-start | bytes 24584 | tf_op jit(solution)/shard_map/ppermute | solution.py:28
  55.9 7.2 %collective-permute-start.6 = (bf16[8,512]{1,0:T(8,128)(2,1)S(1)}, bf16[8,512]{1,0:T(8,128)(2,1)S(1)}, u32[]{:S(2)}, u32[]{:S(2)}) collective-permute-start(bf16[8,512]{1,0:T(8,128)(2,1)S(1)} %collective-permute-done.4), channel_id=1, source_target_pairs={{0,2},{2,4},{4,6},{6,8},{8,10},{10,12},{12,14},{14,16},{16,18},{18... | collective-permute-start | bytes 24584 | tf_op jit(solution)/shard_map/ppermute | solution.py:23
  55.9 7.2 %collective-permute-start.7 = (bf16[8,512]{1,0:T(8,128)(2,1)S(1)}, bf16[8,512]{1,0:T(8,128)(2,1)S(1)}, u32[]{:S(2)}, u32[]{:S(2)}) collective-permute-start(bf16[8,512]{1,0:T(8,128)(2,1)S(1)} %collective-permute-done.5), channel_id=1, source_target_pairs={{0,30},{2,0},{4,2},{6,4},{8,6},{10,8},{12,10},{14,12},{16,14},{18,... | collective-permute-start | bytes 24584 | tf_op jit(solution)/shard_map/ppermute | solution.py:28
  63.1 7.2 %collective-permute-start.8 = (bf16[8,512]{1,0:T(8,128)(2,1)S(1)}, bf16[8,512]{1,0:T(8,128)(2,1)S(1)}, u32[]{:S(2)}, u32[]{:S(2)}) collective-permute-start(bf16[8,512]{1,0:T(8,128)(2,1)S(1)} %collective-permute-done.6), channel_id=1, source_target_pairs={{0,2},{2,4},{4,6},{6,8},{8,10},{10,12},{12,14},{14,16},{16,18},{18... | collective-permute-start | bytes 24584 | tf_op jit(solution)/shard_map/ppermute | solution.py:23
  63.1 7.2 %collective-permute-start.9 = (bf16[8,512]{1,0:T(8,128)(2,1)S(1)}, bf16[8,512]{1,0:T(8,128)(2,1)S(1)}, u32[]{:S(2)}, u32[]{:S(2)}) collective-permute-start(bf16[8,512]{1,0:T(8,128)(2,1)S(1)} %collective-permute-done.7), channel_id=1, source_target_pairs={{0,30},{2,0},{4,2},{6,4},{8,6},{10,8},{12,10},{14,12},{16,14},{18,... | collective-permute-start | bytes 24584 | tf_op jit(solution)/shard_map/ppermute | solution.py:28
  70.4 7.2 %collective-permute-start.10 = (bf16[8,512]{1,0:T(8,128)(2,1)S(1)}, bf16[8,512]{1,0:T(8,128)(2,1)S(1)}, u32[]{:S(2)}, u32[]{:S(2)}) collective-permute-start(bf16[8,512]{1,0:T(8,128)(2,1)S(1)} %collective-permute-done.8), channel_id=1, source_target_pairs={{0,2},{2,4},{4,6},{6,8},{8,10},{10,12},{12,14},{14,16},{16,18},{18... | collective-permute-start | bytes 24584 | tf_op jit(solution)/shard_map/ppermute | solution.py:23
  70.4 7.2 %collective-permute-start.11 = (bf16[8,512]{1,0:T(8,128)(2,1)S(1)}, bf16[8,512]{1,0:T(8,128)(2,1)S(1)}, u32[]{:S(2)}, u32[]{:S(2)}) collective-permute-start(bf16[8,512]{1,0:T(8,128)(2,1)S(1)} %collective-permute-done.9), channel_id=1, source_target_pairs={{0,30},{2,0},{4,2},{6,4},{8,6},{10,8},{12,10},{14,12},{16,14},{18,... | collective-permute-start | bytes 24584 | tf_op jit(solution)/shard_map/ppermute | solution.py:28
  77.6 7.2 %collective-permute-start.12 = (bf16[8,512]{1,0:T(8,128)(2,1)S(1)}, bf16[8,512]{1,0:T(8,128)(2,1)S(1)}, u32[]{:S(2)}, u32[]{:S(2)}) collective-permute-start(bf16[8,512]{1,0:T(8,128)(2,1)S(1)} %collective-permute-done.10), channel_id=1, source_target_pairs={{0,2},{2,4},{4,6},{6,8},{8,10},{10,12},{12,14},{14,16},{16,18},{18... | collective-permute-start | bytes 24584 | tf_op jit(solution)/shard_map/ppermute | solution.py:23
  77.6 7.2 %collective-permute-start.13 = (bf16[8,512]{1,0:T(8,128)(2,1)S(1)}, bf16[8,512]{1,0:T(8,128)(2,1)S(1)}, u32[]{:S(2)}, u32[]{:S(2)}) collective-permute-start(bf16[8,512]{1,0:T(8,128)(2,1)S(1)} %collective-permute-done.11), channel_id=1, source_target_pairs={{0,30},{2,0},{4,2},{6,4},{8,6},{10,8},{12,10},{14,12},{16,14},{18,... | collective-permute-start | bytes 24584 | tf_op jit(solution)/shard_map/ppermute | solution.py:28
  84.9 7.2 %collective-permute-start.14 = (bf16[8,512]{1,0:T(8,128)(2,1)S(1)}, bf16[8,512]{1,0:T(8,128)(2,1)S(1)}, u32[]{:S(2)}, u32[]{:S(2)}) collective-permute-start(bf16[8,512]{1,0:T(8,128)(2,1)S(1)} %collective-permute-done.12), channel_id=1, source_target_pairs={{0,2},{2,4},{4,6},{6,8},{8,10},{10,12},{12,14},{14,16},{16,18},{18... | collective-permute-start | bytes 24584 | tf_op jit(solution)/shard_map/ppermute | solution.py:23
  84.9 7.2 %collective-permute-start.15 = (bf16[8,512]{1,0:T(8,128)(2,1)S(1)}, bf16[8,512]{1,0:T(8,128)(2,1)S(1)}, u32[]{:S(2)}, u32[]{:S(2)}) collective-permute-start(bf16[8,512]{1,0:T(8,128)(2,1)S(1)} %collective-permute-done.13), channel_id=1, source_target_pairs={{0,30},{2,0},{4,2},{6,4},{8,6},{10,8},{12,10},{14,12},{16,14},{18,... | collective-permute-start | bytes 24584 | tf_op jit(solution)/shard_map/ppermute | solution.py:28
  92.1 7.2 %collective-permute-start.16 = (bf16[8,512]{1,0:T(8,128)(2,1)S(1)}, bf16[8,512]{1,0:T(8,128)(2,1)S(1)}, u32[]{:S(2)}, u32[]{:S(2)}) collective-permute-start(bf16[8,512]{1,0:T(8,128)(2,1)S(1)} %collective-permute-done.14), channel_id=1, source_target_pairs={{0,2},{2,4},{4,6},{6,8},{8,10},{10,12},{12,14},{14,16},{16,18},{18... | collective-permute-start | bytes 24584 | tf_op jit(solution)/shard_map/ppermute | solution.py:23
  99.9 16.3 %copy-start.22 = (f32[256]{0:T(256)S(1)}, f32[256]{0:T(256)}, u32[]{:S(2)}) copy-start(f32[256]{0:T(256)} %param.22) | copy-start | bytes 3076
  121.1 1.3 copy-start.3
  122.4 8.5 %copy-start.20 = (s32[32]{0:T(128)S(1)}, s32[32]{0:T(128)}, u32[]{:S(2)}) copy-start(s32[32]{0:T(128)} %param.31) | copy-start | bytes 388
  131.0 14.4 %copy-start.10 = (bf16[512,256]{1,0:T(8,128)(2,1)S(1)}, bf16[512,256]{1,0:T(8,128)(2,1)}, u32[]{:S(2)}) copy-start(bf16[512,256]{1,0:T(8,128)(2,1)} %param.25) | copy-start | bytes 786436
  131.0 14.4 %copy-start.21 = (f32[256]{0:T(256)S(1)}, f32[256]{0:T(256)}, u32[]{:S(2)}) copy-start(f32[256]{0:T(256)} %param.26) | copy-start | bytes 3076
  138.7 9.5 %copy-start.24 = (s32[3]{0:T(128)S(1)}, s32[3]{0:T(128)}, u32[]{:S(2)}) copy-start(s32[3]{0:T(128)} %constant.170.clone.1) | copy-start | bytes 40
  145.4 21.8 %copy-start.5 = (bf16[512,512]{1,0:T(8,128)(2,1)S(1)}, bf16[512,512]{1,0:T(8,128)(2,1)}, u32[]{:S(2)}) copy-start(bf16[512,512]{1,0:T(8,128)(2,1)} %param.35) | copy-start | bytes 1572868
  145.4 21.8 %copy-start.19 = (f32[512]{0:T(512)S(1)}, f32[512]{0:T(512)}, u32[]{:S(2)}) copy-start(f32[512]{0:T(512)} %param.28) | copy-start | bytes 6148
  145.4 23.6 %copy-start.1 = (bf16[512,512]{1,0:T(8,128)(2,1)S(1)}, bf16[512,512]{1,0:T(8,128)(2,1)}, u32[]{:S(2)}) copy-start(bf16[512,512]{1,0:T(8,128)(2,1)} %param.19) | copy-start | bytes 1572868
  145.7 3.3 copy-start.13
  148.2 151.4 %reduce-scatter.3.cloned.1.call-start = ((), (), s32[]{:S(2)}) async-start(), calls=%async_computation.3 | async-start | bytes 139264 | tf_op jit(solution)/shard_map/reduce_scatter | solution.py:173
  164.1 4.9 %copy-start.2 = (f32[512,512]{1,0:T(8,128)S(1)}, f32[512,512]{1,0:T(8,128)}, u32[]{:S(2)}) copy-start(f32[512,512]{1,0:T(8,128)} %all-reduce.7.cloned.1.call-done) | copy-start | bytes 3145732
  164.1 6.2 %copy-start.14 = (f32[512,256]{1,0:T(8,128)S(1)}, f32[512,256]{1,0:T(8,128)}, u32[]{:S(2)}) copy-start(f32[512,256]{1,0:T(8,128)} %copy-done.13) | copy-start | bytes 1572868
  165.6 4.7 copy-start.25
  170.3 1.6 copy-start.11
  170.3 3.0 copy-start.12
  170.6 2.7 copy-start.7
  209.1 2.7 copy-start.23
  215.8 15.2 %collective-permute-start.17 = (bf16[128,256]{1,0:T(8,128)(2,1)S(1)}, bf16[128,256]{1,0:T(8,128)(2,1)S(1)}, u32[]{:S(2)}, u32[]{:S(2)}) collective-permute-start(bf16[128,256]{1,0:T(8,128)(2,1)S(1)} %bitcast.97), channel_id=1, source_target_pairs={{2,0},{4,2},{6,4},{8,6},{10,8},{12,10},{14,12},{16,14},{18,16},{20... | collective-permute-start | bytes 196616 | tf_op jit(solution)/shard_map/ppermute | solution.py:41
  221.4 9.7 %collective-permute-start.18 = (bf16[128,256]{1,0:T(8,128)(2,1)S(1)}, bf16[128,256]{1,0:T(8,128)(2,1)S(1)}, u32[]{:S(2)}, u32[]{:S(2)}) collective-permute-start(bf16[128,256]{1,0:T(8,128)(2,1)S(1)} %bitcast.98), channel_id=1, source_target_pairs={{30,0},{0,2},{2,4},{4,6},{6,8},{8,10},{10,12},{12,14},{14,16},{16,... | collective-permute-start | bytes 196616 | tf_op jit(solution)/shard_map/ppermute | solution.py:41
  222.3 130.8 %reduce-scatter.5.cloned.1.call-start = ((), (), s32[]{:S(2)}) async-start(), calls=%async_computation.4 | async-start | bytes 786432 | tf_op jit(solution)/shard_map/reduce_scatter | solution.py:186
  232.9 73.7 %copy-start.4 = (bf16[4096,256]{1,0:T(8,128)(2,1)S(1)}, bf16[4096,256]{1,0:T(8,128)(2,1)}, u32[]{:S(2)}) copy-start(bf16[4096,256]{1,0:T(8,128)(2,1)} %copy-done.3) | copy-start | bytes 6291460
  304.5 163.1 %all-reduce.9.cloned.1.call-start = ((), (), s32[]{:S(2)}) async-start(), calls=%async_computation.5 | async-start | bytes 6291456 | tf_op jit(solution)/shard_map/psum | solution.py:192
  311.1 1.2 copy-start.6
  467.6 4.3 copy-start.18
  467.6 5.4 %copy-start.17 = (f32[512,256]{0,1:T(8,128)S(1)}, f32[512,256]{0,1:T(8,128)}, u32[]{:S(2)}) copy-start(f32[512,256]{0,1:T(8,128)} %get-tuple-element.88) | copy-start | bytes 1572868
  467.6 6.4 %copy-start.16 = (f32[256,512]{1,0:T(8,128)S(1)}, f32[256,512]{1,0:T(8,128)}, u32[]{:S(2)}) copy-start(f32[256,512]{1,0:T(8,128)} %get-tuple-element.89) | copy-start | bytes 1572868
  468.8 6.1 %copy-start.15 = (f32[256,512]{1,0:T(8,128)S(1)}, f32[256,512]{1,0:T(8,128)}, u32[]{:S(2)}) copy-start(f32[256,512]{1,0:T(8,128)} %get-tuple-element.86) | copy-start | bytes 1572868
  (1 other events, 0.7 us)
Sparse Core Ops, SparseCore 0:
  148.3 15.7 all-reduce.6
  222.4 77.1 reduce-scatter.2
  304.6 4.2 reduce-scatter.4
  316.9 150.6 all-reduce.8
